TPU v7x, 256 devices: a whole 4x4x8 slice. The times are simulated.
256 devices in a mesh: row: 8 (over x, core), col: 32 (over y, z).
Axes of the slice: x: 4, y: 4, z: 8, core: 2. Of those that a mesh axis runs over, the one named last changes fastest.
Arguments:
- src_coords: int32 [3, 131072], P(None, 'row'), may hold values from 0 to 51
- tgt_coords: int32 [3, 262144], P(None, 'col'), may hold values from 0 to 51
- src_mass: int32 [131072], P('row'), may hold values from 1 to 298
- tgt_mass: int32 [262144], P('col'), may hold values from 1 to 298
- tgt_start: float32 [262144], P('col'), may hold values from -10 to 170
- kept_src: int32 [8, 32, 64], P('row', 'col'), may hold values from 0 to 127, as said below
- kept_tgt: int32 [8, 32, 64], P('row', 'col'), may hold values from 0 to 63, as said below
- kept_count: int32 [8, 32], P('row', 'col'), may hold values from 1 to 64, as said below
Outputs:
- src_potential: float32 [131072], P('row')
- tgt_potential: float32 [262144], P('col')
Inputs may be any that keep to these rules, and one draw needn't show every extreme that they name: `kept_src`: every source tile lies in a live pair of some device of its row block. Slots at or past a device's count hold pairs that are not live. `kept_tgt`: every target tile lies in a live pair of some device of its column block. `kept_count`: some device has exactly 64 live slots in every draw.
All inputs are finite; a program needn't handle non-finite values.
Results may differ from a plain program's by a relative error of at most 0.0001.
Values sent between devices are 32-bit elements; how exact they have to be, the bound alone decides.
No kernel may reach another device: no remote copies, remote signals or barrier semaphores. Data moves between devices by JAX's collectives and lax.ppermute only.
A program may use at most 64 MiB of HBM per device.

v0:
```python
import jax
import jax.numpy as jnp
from jax import lax
from jax.sharding import PartitionSpec as P

ITERS = 3
very_negative = -1e30
cost_scale = 0.05


def tile_costs(src_coords, tgt_coords, src_ids, tgt_ids):
    src_tiles = jnp.take(src_coords.reshape(3, -1, 128), src_ids, axis=1).astype(jnp.float32)
    tgt_tiles = jnp.take(tgt_coords.reshape(3, -1, 128), tgt_ids, axis=1).astype(jnp.float32)
    square = None
    for component in range(3):
        difference = src_tiles[component][:, :, None] - tgt_tiles[component][:, None, :]
        square = difference * difference if component == 0 else square + difference * difference
    return cost_scale * square


def slot_partials(scores, live_slots, reduce_dim):
    peak_values = jnp.max(scores, axis=reduce_dim)
    totals = jnp.sum(jnp.exp(scores - jnp.expand_dims(peak_values, reduce_dim)), axis=reduce_dim)
    return (
        jnp.where(live_slots[:, None], peak_values, very_negative),
        jnp.where(live_slots[:, None], totals, 0.0),
    )


def fold_tiles(peak_values, totals, tile_ids, tile_count):
    member = tile_ids[:, None] == jnp.arange(tile_count, dtype=jnp.int32)[None, :]
    tile_peak = jnp.max(
        jnp.where(member[:, :, None], peak_values[:, None, :], very_negative), axis=0
    )
    slot_peak = jnp.take(tile_peak, tile_ids, axis=0)
    weighted = totals * jnp.exp(peak_values - slot_peak)
    tile_total = jnp.dot(member.astype(jnp.float32).T, weighted, precision=lax.Precision.HIGHEST)
    return (tile_peak.reshape(-1), tile_total.reshape(-1))


def row_merge(tile_peak, tile_total, src_log):
    highest = lax.pmax(tile_peak, "col")
    summed = lax.psum(tile_total * jnp.exp(tile_peak - highest), "col")
    return src_log - (highest + jnp.log(summed))


def col_merge(tile_peak, tile_total, tgt_log):
    highest = lax.pmax(tile_peak, "row")
    summed = lax.psum(tile_total * jnp.exp(tile_peak - highest), "row")
    return tgt_log - (highest + jnp.log(summed))


def on_device(
    src_coords, tgt_coords, src_mass, tgt_mass, tgt_start, kept_src, kept_tgt, kept_count
):
    src_ids = kept_src[0, 0]
    tgt_ids = kept_tgt[0, 0]
    live_slots = jnp.arange(src_ids.shape[0], dtype=jnp.int32) < kept_count[0, 0]
    src_tiles_count = src_coords.shape[1] // 128
    tgt_tiles_count = tgt_coords.shape[1] // 128
    src_weight = src_mass.astype(jnp.float32)
    tgt_weight = tgt_mass.astype(jnp.float32)
    src_sum = lax.psum(jnp.sum(src_weight), "row")
    tgt_sum = lax.psum(jnp.sum(tgt_weight), "col")
    src_log = jnp.log(src_weight) - jnp.log(src_sum)
    tgt_log = jnp.log(tgt_weight) - jnp.log(tgt_sum)
    cost = tile_costs(src_coords, tgt_coords, src_ids, tgt_ids)
    tgt_potential = tgt_start
    src_potential = None
    for iteration in range(ITERS):
        tgt_picked = jnp.take(tgt_potential.reshape(-1, 128), tgt_ids, axis=0)
        peak_values, totals = slot_partials(tgt_picked[:, None, :] - cost, live_slots, 2)
        tile_peak, tile_total = fold_tiles(peak_values, totals, src_ids, src_tiles_count)
        src_potential = row_merge(tile_peak, tile_total, src_log)
        src_picked = jnp.take(src_potential.reshape(-1, 128), src_ids, axis=0)
        peak_values, totals = slot_partials(src_picked[:, :, None] - cost, live_slots, 1)
        tile_peak, tile_total = fold_tiles(peak_values, totals, tgt_ids, tgt_tiles_count)
        tgt_potential = col_merge(tile_peak, tile_total, tgt_log)
    return (src_potential, tgt_potential)


def solution(mesh):
    placed = (
        P(None, "row"),
        P(None, "col"),
        P("row"),
        P("col"),
        P("col"),
        P("row", "col", None),
        P("row", "col", None),
        P("row", "col"),
    )
    return jax.shard_map(
        on_device, mesh=mesh, in_specs=placed, out_specs=(P("row"), P("col")), check_vma=False
    )
```

profile of v0, /device:TPU:8, one launch (start us, length us, event | category | flops | bytes accessed | tf_op | source)
XLA Modules:
  0.0 1064.5 jit_solution(4097321126829979318)
XLA Ops:
  15.0 5.1 subtract_reduce_fusion.5
  20.2 2.0 select_reduce_fusion.2
  22.3 6.4 exponential_reduce_fusion.5
  30.8 133.8 %all-reduce.7.cloned.1.call-done = f32[16384]{0:T(1024)} async-done(((f32[16384]{0:T(1024)}), f32[16384]{0:T(1024)}) %all-reduce.7.cloned.1.call-update) | async-done | bytes 65552 | tf_op jit(solution)/shard_map/pmax | solution.py:42
  164.6 1.9 fusion
  166.6 61.8 %psum.57 = f32[]{:T(128)} all-reduce(f32[]{:T(128)} %convert_reduce_fusion.1), channel_id=1, replica_groups=mesh['row'=8,'col'=32] {'col'}, use_global_device_ids=true, to_apply=%region_3.0 | all-reduce | flops 1 | bytes 8 | tf_op jit(solution)/shard_map/psum | solution.py:64
  228.4 13.1 %psum.56 = f32[]{:T(128)} all-reduce(f32[]{:T(128)} %convert_reduce_fusion), channel_id=1, replica_groups=mesh['row'=8,'col'=32] {'row'}, use_global_device_ids=true, to_apply=%region_1.0 | all-reduce | flops 1 | bytes 8 | tf_op jit(solution)/shard_map/psum | solution.py:63
  242.8 63.6 %all-reduce.9.cloned.1.call-done = f32[16384]{0:T(1024)} async-done(((f32[16384]{0:T(1024)}), f32[16384]{0:T(1024)}) %all-reduce.9.cloned.1.call-update) | async-done | bytes 65552 | tf_op jit(solution)/shard_map/psum | solution.py:43
  307.9 5.0 subtract_reduce_fusion.4
  312.9 5.1 exponential_reduce_fusion.4
  319.3 23.6 %pmax.43 = f32[8192]{0:T(1024)S(1)} all-reduce(f32[8192]{0:T(1024)S(1)} %bitcast.78), channel_id=1, replica_groups=mesh['row'=8,'col'=32] {'row'}, use_global_device_ids=true, to_apply=%region_11.14 | all-reduce | flops 8192 | bytes 65536 | tf_op jit(solution)/shard_map/pmax | solution.py:48
  343.2 23.6 %psum.59 = f32[8192]{0:T(1024)S(1)} all-reduce(f32[8192]{0:T(1024)S(1)} %fusion.3), channel_id=1, replica_groups=mesh['row'=8,'col'=32] {'row'}, use_global_device_ids=true, to_apply=%region_13.16 | all-reduce | flops 8192 | bytes 65536 | tf_op jit(solution)/shard_map/psum | solution.py:49
  367.5 5.1 subtract_reduce_fusion.3
  372.7 2.0 select_reduce_fusion.1
  374.8 6.4 exponential_reduce_fusion.3
  381.9 128.1 %all-reduce.11.cloned.1.call-done = f32[16384]{0:T(1024)} async-done(((f32[16384]{0:T(1024)}), f32[16384]{0:T(1024)}) %all-reduce.11.cloned.1.call-update) | async-done | bytes 65552 | tf_op jit(solution)/shard_map/pmax | solution.py:42
  510.0 1.9 fusion.1
  512.0 139.3 %all-reduce.13.cloned.1.call-done = f32[16384]{0:T(1024)} async-done(((f32[16384]{0:T(1024)}), f32[16384]{0:T(1024)}) %all-reduce.13.cloned.1.call-update) | async-done | bytes 65552 | tf_op jit(solution)/shard_map/psum | solution.py:43
  652.8 5.0 subtract_reduce_fusion.2
  657.7 5.1 exponential_reduce_fusion.2
  664.2 23.6 %pmax.45 = f32[8192]{0:T(1024)S(1)} all-reduce(f32[8192]{0:T(1024)S(1)} %bitcast.79), channel_id=1, replica_groups=mesh['row'=8,'col'=32] {'row'}, use_global_device_ids=true, to_apply=%region_21.24 | all-reduce | flops 8192 | bytes 65536 | tf_op jit(solution)/shard_map/pmax | solution.py:48
  688.1 23.6 %psum.61 = f32[8192]{0:T(1024)S(1)} all-reduce(f32[8192]{0:T(1024)S(1)} %fusion.4), channel_id=1, replica_groups=mesh['row'=8,'col'=32] {'row'}, use_global_device_ids=true, to_apply=%region_23.26 | all-reduce | flops 8192 | bytes 65536 | tf_op jit(solution)/shard_map/psum | solution.py:49
  712.4 5.1 subtract_reduce_fusion.1
  717.6 2.0 select_reduce_fusion
  719.9 6.4 exponential_reduce_fusion.1
  726.9 128.0 %all-reduce.15.cloned.1.call-done = f32[16384]{0:T(1024)} async-done(((f32[16384]{0:T(1024)}), f32[16384]{0:T(1024)}) %all-reduce.15.cloned.1.call-update) | async-done | bytes 65552 | tf_op jit(solution)/shard_map/pmax | solution.py:42
  854.9 1.9 fusion.2
  856.8 139.7 %all-reduce.17.cloned.1.call-done = f32[16384]{0:T(1024)} async-done(((f32[16384]{0:T(1024)}), f32[16384]{0:T(1024)}) %all-reduce.17.cloned.1.call-update) | async-done | bytes 65552 | tf_op jit(solution)/shard_map/psum | solution.py:43
  998.1 5.0 subtract_reduce_fusion
  1003.1 5.1 exponential_reduce_fusion
  1009.5 23.6 %pmax.47 = f32[8192]{0:T(1024)S(1)} all-reduce(f32[8192]{0:T(1024)S(1)} %bitcast.77), channel_id=1, replica_groups=mesh['row'=8,'col'=32] {'row'}, use_global_device_ids=true, to_apply=%region_31.34 | all-reduce | flops 8192 | bytes 65536 | tf_op jit(solution)/shard_map/pmax | solution.py:48
  1033.4 23.6 %psum.63 = f32[8192]{0:T(1024)S(1)} all-reduce(f32[8192]{0:T(1024)S(1)} %fusion.5), channel_id=1, replica_groups=mesh['row'=8,'col'=32] {'row'}, use_global_device_ids=true, to_apply=%region_33.36 | all-reduce | flops 8192 | bytes 65536 | tf_op jit(solution)/shard_map/psum | solution.py:49
  (96 shorter events, 22.7 us)
Async XLA Ops:
  7.2 4.1 copy-start
  7.2 157.4 %all-reduce.7.cloned.1.call-start = ((), (), s32[]{:S(2)}) async-start(), calls=%async_computation | async-start | bytes 131072 | tf_op jit(solution)/shard_map/pmax | solution.py:42
  11.9 0.9 copy-start.11
  13.5 0.8 copy-start.4
  13.6 1.3 copy-start.12
  22.2 6.5 copy-start.1
  22.3 284.1 %all-reduce.9.cloned.1.call-start = ((), (), s32[]{:S(2)}) async-start(), calls=%async_computation.1 | async-start | bytes 131072 | tf_op jit(solution)/shard_map/psum | solution.py:43
  28.7 0.8 copy-start.6
  28.7 1.4 copy-start.7
  29.6 136.9 %copy-start.13 = (s32[1,1,64]{2,1,0:T(1,128)S(1)}, s32[1,1,64]{2,1,0:T(1,128)}, u32[]{:S(2)}) copy-start(s32[1,1,64]{2,1,0:T(1,128)} %param.18) | copy-start | bytes 772
  164.6 141.8 %copy-start.8 = (f32[16384]{0:T(1024)S(1)}, f32[16384]{0:T(1024)}, u32[]{:S(2)}) copy-start(f32[16384]{0:T(1024)} %all-reduce.7.cloned.1.call-done) | copy-start | bytes 196612
  166.5 343.6 %all-reduce.11.cloned.1.call-start = ((), (), s32[]{:S(2)}) async-start(), calls=%async_computation.2 | async-start | bytes 131072 | tf_op jit(solution)/shard_map/pmax | solution.py:42
  374.8 6.5 copy-start.3
  374.8 276.4 %all-reduce.13.cloned.1.call-start = ((), (), s32[]{:S(2)}) async-start(), calls=%async_computation.3 | async-start | bytes 131072 | tf_op jit(solution)/shard_map/psum | solution.py:43
  510.0 141.2 %copy-start.9 = (f32[16384]{0:T(1024)S(1)}, f32[16384]{0:T(1024)}, u32[]{:S(2)}) copy-start(f32[16384]{0:T(1024)} %all-reduce.11.cloned.1.call-done) | copy-start | bytes 196612
  511.9 343.0 %all-reduce.15.cloned.1.call-start = ((), (), s32[]{:S(2)}) async-start(), calls=%async_computation.4 | async-start | bytes 131072 | tf_op jit(solution)/shard_map/pmax | solution.py:42
  719.7 6.7 copy-start.2
  719.7 276.8 %all-reduce.17.cloned.1.call-start = ((), (), s32[]{:S(2)}) async-start(), calls=%async_computation.5 | async-start | bytes 131072 | tf_op jit(solution)/shard_map/psum | solution.py:43
  854.9 141.6 %copy-start.10 = (f32[16384]{0:T(1024)S(1)}, f32[16384]{0:T(1024)}, u32[]{:S(2)}) copy-start(f32[16384]{0:T(1024)} %all-reduce.15.cloned.1.call-done) | copy-start | bytes 196612
  997.4 5.7 copy-start.5
Sparse Core Ops, SparseCore 0:
  22.4 142.1 all-reduce.6
  169.0 137.2 all-reduce.8
  374.9 135.0 all-reduce.10
  513.9 137.2 all-reduce.12
  719.8 135.0 all-reduce.14
  859.2 137.2 all-reduce.16
where the time goes:
time: 1070 us; the launch traced here: 1060 us
  waiting for transfers between devices  733 us (69%)
  blocking collectives  216 us (20%)
  other arithmetic  82.2 us (8%)
  between operations  16.4 us (2%)
    pmax x3, waiting for transfers between devices, row_merge(): highest = lax.pmax(tile_peak, 'col')  390 us
    psum x3, waiting for transfers between devices, row_merge(): summed = lax.psum(tile_total * jnp.exp(tile_peak - highest), 'col')  343 us
    psum x3, blocking collectives, col_merge(): summed = lax.psum(tile_total * jnp.exp(tile_peak - highest), 'row')  70.8 us
    pmax x3, blocking collectives, col_merge(): highest = lax.pmax(tile_peak, 'row')  70.8 us
    psum x1, blocking collectives, on_device(): tgt_sum = lax.psum(jnp.sum(tgt_weight), 'col')  61.8 us
    reduce_sum x6, other arithmetic, slot_partials(): jnp.sum(jnp.exp(scores - jnp.expand_dims(peak_values, reduce_dim)), axis=...  34.4 us
    reduce_max x6, other arithmetic, slot_partials(): peak_values = jnp.max(scores, axis=reduce_dim)  30.4 us
  transfers between devices with their start and end apart: 6, of which 6 were waited for; matrix products, arithmetic and copies ran while one was open for 2% of the time, Pallas kernels for 0%

commit v1 on v0

--- a/solution.py
+++ b/solution.py
@@ -40,7 +40,8 @@
 
 def row_merge(tile_peak, tile_total, src_log):
     highest = lax.pmax(tile_peak, "col")
-    summed = lax.psum(tile_total * jnp.exp(tile_peak - highest), "col")
+    body = tile_total * jnp.exp(tile_peak - highest)
+    summed = jnp.sum(lax.all_gather(body, axis_name="col"), axis=0)
     return src_log - (highest + jnp.log(summed))
 
 

time: 1070 us -> 890 us (0.83)
  waiting for transfers between devices: 733 us -> 551 us
    psum x3 -> x0, waiting for transfers between devices: 343 us -> none  [row_merge(): summed = lax.psum(tile_total * jnp.exp(tile_peak - highest), 'col')]
    all_gather x0 -> x3, waiting for transfers between devices: none -> 153 us  [row_merge(): summed = jnp.sum(lax.all_gather(body, axis_name='col'), axis=0)]
  transfers between devices with their start and end apart: 6 -> 6, of which waited for: 6 -> 5; matrix products, arithmetic and copies ran while one was open for 2% -> 3% of each run, Pallas kernels for 0% -> 0%
where the time goes in v1:
time: 890 us; the launch traced here: 889 us
  waiting for transfers between devices  551 us (62%)
  blocking collectives  217 us (24%)
  other arithmetic  81 us (9%)
  local copies, waits for them, and re-layouts  17.5 us (2%)
  between operations  16.5 us (2%)
    pmax x3, waiting for transfers between devices, row_merge(): highest = lax.pmax(tile_peak, 'col')  398 us
    all_gather x3, waiting for transfers between devices, row_merge(): summed = jnp.sum(lax.all_gather(body, axis_name='col'), axis=0)  153 us
    psum x3, blocking collectives, col_merge(): summed = lax.psum(tile_total * jnp.exp(tile_peak - highest), 'row')  71 us
    pmax x3, blocking collectives, col_merge(): highest = lax.pmax(tile_peak, 'row')  70.8 us
    psum x1, blocking collectives, on_device(): tgt_sum = lax.psum(jnp.sum(tgt_weight), 'col')  61.9 us
    reduce_sum x6, other arithmetic, slot_partials(): jnp.sum(jnp.exp(scores - jnp.expand_dims(peak_values, reduce_dim)), axis=...  34.5 us
    reduce_max x6, other arithmetic, slot_partials(): peak_values = jnp.max(scores, axis=reduce_dim)  30.4 us
  transfers between devices with their start and end apart: 6, of which 5 were waited for; matrix products, arithmetic and copies ran while one was open for 3% of the time, Pallas kernels for 0%

profile of v1, /device:TPU:8, one launch (start us, length us, event | category | flops | bytes accessed | tf_op | source)
XLA Modules:
  0.0 889.3 jit_solution(5867446443278503430)
XLA Ops:
  16.2 5.1 subtract_reduce_fusion.5
  21.4 2.0 select_reduce_fusion.2
  23.5 6.4 exponential_reduce_fusion.5
  30.6 135.1 %all-reduce.4.cloned.1.call-done = f32[16384]{0:T(1024)} async-done(((f32[16384]{0:T(1024)}), f32[16384]{0:T(1024)}) %all-reduce.4.cloned.1.call-update) | async-done | bytes 65552 | tf_op jit(solution)/shard_map/pmax | solution.py:42
  165.7 1.8 fusion
  168.9 61.9 %psum.36 = f32[]{:T(128)} all-reduce(f32[]{:T(128)} %convert_reduce_fusion.1), channel_id=1, replica_groups=mesh['row'=8,'col'=32] {'col'}, use_global_device_ids=true, to_apply=%region_3.0 | all-reduce | flops 1 | bytes 8 | tf_op jit(solution)/shard_map/psum | solution.py:65
  230.8 13.3 %psum.35 = f32[]{:T(128)} all-reduce(f32[]{:T(128)} %convert_reduce_fusion), channel_id=1, replica_groups=mesh['row'=8,'col'=32] {'row'}, use_global_device_ids=true, to_apply=%region_1.0 | all-reduce | flops 1 | bytes 8 | tf_op jit(solution)/shard_map/psum | solution.py:64
  245.5 1.8 reshape.428
  248.8 5.0 subtract_reduce_fusion.4
  253.8 5.1 exponential_reduce_fusion.4
  260.3 23.6 %pmax.43 = f32[8192]{0:T(1024)S(1)} all-reduce(f32[8192]{0:T(1024)S(1)} %bitcast.78), channel_id=1, replica_groups=mesh['row'=8,'col'=32] {'row'}, use_global_device_ids=true, to_apply=%region_11.14 | all-reduce | flops 8192 | bytes 65536 | tf_op jit(solution)/shard_map/pmax | solution.py:49
  284.1 23.6 %psum.37 = f32[8192]{0:T(1024)S(1)} all-reduce(f32[8192]{0:T(1024)S(1)} %fusion.3), channel_id=1, replica_groups=mesh['row'=8,'col'=32] {'row'}, use_global_device_ids=true, to_apply=%region_13.16 | all-reduce | flops 8192 | bytes 65536 | tf_op jit(solution)/shard_map/psum | solution.py:50
  308.4 5.1 subtract_reduce_fusion.3
  313.7 2.0 select_reduce_fusion.1
  315.8 6.4 exponential_reduce_fusion.3
  322.8 134.6 %all-reduce.6.cloned.1.call-done = f32[16384]{0:T(1024)} async-done(((f32[16384]{0:T(1024)}), f32[16384]{0:T(1024)}) %all-reduce.6.cloned.1.call-update) | async-done | bytes 65552 | tf_op jit(solution)/shard_map/pmax | solution.py:42
  457.4 1.8 fusion.1
  459.2 76.2 %all-gather.9.cloned.1.call-done = f32[524288]{0:T(1024)} async-done(((f32[16384]{0:T(1024)}), f32[524288]{0:T(1024)}) %all-gather.9.cloned.1.call-update) | async-done | bytes 2097168 | tf_op jit(solution)/shard_map/all_gather | solution.py:44
  538.8 5.0 subtract_reduce_fusion.2
  543.8 5.1 exponential_reduce_fusion.2
  550.2 23.6 %pmax.45 = f32[8192]{0:T(1024)S(1)} all-reduce(f32[8192]{0:T(1024)S(1)} %bitcast.79), channel_id=1, replica_groups=mesh['row'=8,'col'=32] {'row'}, use_global_device_ids=true, to_apply=%region_21.24 | all-reduce | flops 8192 | bytes 65536 | tf_op jit(solution)/shard_map/pmax | solution.py:49
  574.1 23.8 %psum.38 = f32[8192]{0:T(1024)S(1)} all-reduce(f32[8192]{0:T(1024)S(1)} %fusion.4), channel_id=1, replica_groups=mesh['row'=8,'col'=32] {'row'}, use_global_device_ids=true, to_apply=%region_23.26 | all-reduce | flops 8192 | bytes 65536 | tf_op jit(solution)/shard_map/psum | solution.py:50
  598.6 5.1 subtract_reduce_fusion.1
  603.8 2.0 select_reduce_fusion
  605.9 6.4 exponential_reduce_fusion.1
  613.0 128.2 %all-reduce.8.cloned.1.call-done = f32[16384]{0:T(1024)} async-done(((f32[16384]{0:T(1024)}), f32[16384]{0:T(1024)}) %all-reduce.8.cloned.1.call-update) | async-done | bytes 65552 | tf_op jit(solution)/shard_map/pmax | solution.py:42
  741.1 1.8 fusion.2
  742.9 76.6 %all-gather.11.cloned.1.call-done = f32[524288]{0:T(1024)} async-done(((f32[16384]{0:T(1024)}), f32[524288]{0:T(1024)}) %all-gather.11.cloned.1.call-update) | async-done | bytes 2097168 | tf_op jit(solution)/shard_map/all_gather | solution.py:44
  822.9 5.0 subtract_reduce_fusion
  827.9 5.1 exponential_reduce_fusion
  834.3 23.6 %pmax.47 = f32[8192]{0:T(1024)S(1)} all-reduce(f32[8192]{0:T(1024)S(1)} %bitcast.77), channel_id=1, replica_groups=mesh['row'=8,'col'=32] {'row'}, use_global_device_ids=true, to_apply=%region_31.34 | all-reduce | flops 8192 | bytes 65536 | tf_op jit(solution)/shard_map/pmax | solution.py:49
  858.2 23.6 %psum.39 = f32[8192]{0:T(1024)S(1)} all-reduce(f32[8192]{0:T(1024)S(1)} %fusion.5), channel_id=1, replica_groups=mesh['row'=8,'col'=32] {'row'}, use_global_device_ids=true, to_apply=%region_33.36 | all-reduce | flops 8192 | bytes 65536 | tf_op jit(solution)/shard_map/psum | solution.py:50
  (98 shorter events, 27.0 us)
Async XLA Ops:
  7.2 4.8 copy-start
  7.2 16.3 %copy-start.10 = (s32[1,1,64]{2,1,0:T(1,128)S(1)}, s32[1,1,64]{2,1,0:T(1,128)}, u32[]{:S(2)}) copy-start(s32[1,1,64]{2,1,0:T(1,128)} %param.17) | copy-start | bytes 772
  7.2 158.5 %all-reduce.4.cloned.1.call-start = ((), (), s32[]{:S(2)}) async-start(), calls=%async_computation | async-start | bytes 131072 | tf_op jit(solution)/shard_map/pmax | solution.py:42
  12.9 154.7 %copy-start.6 = (s32[8192]{0:T(1024)S(1)}, s32[8192]{0:T(1024)}, u32[]{:S(2)}) copy-start(s32[8192]{0:T(1024)} %param.15) | copy-start | bytes 98308
  12.9 155.4 %copy-start.5 = (s32[16384]{0:T(1024)S(1)}, s32[16384]{0:T(1024)}, u32[]{:S(2)}) copy-start(s32[16384]{0:T(1024)} %param.14) | copy-start | bytes 196612
  12.9 232.5 %copy-start.11 = (s32[1,1,64]{2,1,0:T(1,128)S(1)}, s32[1,1,64]{2,1,0:T(1,128)}, u32[]{:S(2)}) copy-start(s32[1,1,64]{2,1,0:T(1,128)} %param.18) | copy-start | bytes 772
  23.4 6.5 copy-start.1
  23.5 222.0 %all-gather.7.cloned.1.call-start = ((), (), s32[]{:S(2)}) async-start(), calls=%async_computation.3 | async-start | bytes 2162688 | tf_op jit(solution)/shard_map/all_gather | solution.py:44
  167.5 289.8 %all-reduce.6.cloned.1.call-start = ((), (), s32[]{:S(2)}) async-start(), calls=%async_computation.1 | async-start | bytes 131072 | tf_op jit(solution)/shard_map/pmax | solution.py:42
  247.3 0.8 copy-start.7
  315.7 6.5 copy-start.3
  315.7 219.8 %all-gather.9.cloned.1.call-start = ((), (), s32[]{:S(2)}) async-start(), calls=%async_computation.4 | async-start | bytes 2162688 | tf_op jit(solution)/shard_map/all_gather | solution.py:44
  459.2 281.9 %all-reduce.8.cloned.1.call-start = ((), (), s32[]{:S(2)}) async-start(), calls=%async_computation.2 | async-start | bytes 131072 | tf_op jit(solution)/shard_map/pmax | solution.py:42
  537.2 0.8 copy-start.8
  605.8 6.5 copy-start.2
  605.9 213.7 %all-gather.11.cloned.1.call-start = ((), (), s32[]{:S(2)}) async-start(), calls=%async_computation.5 | async-start | bytes 2162688 | tf_op jit(solution)/shard_map/all_gather | solution.py:44
  821.3 0.8 copy-start.9
  822.2 60.3 %copy-start.4 = (f32[16384]{0:T(1024)}, f32[16384]{0:T(1024)S(1)}, u32[]{:S(2)}) copy-start(f32[16384]{0:T(1024)S(1)} %add_subtract_fusion) | copy-start | bytes 196612
Sparse Core Ops, SparseCore 0:
  23.6 142.0 all-reduce.3
  169.2 75.0 all-gather.6
  315.8 141.4 all-reduce.5
  460.4 75.0 all-gather.8
  606.0 135.0 all-reduce.7
  744.5 75.0 all-gather.10
